TPU v7x, 512 devices: a whole 4x8x8 slice. The times are simulated.
512 devices in a mesh: dp: 4 (over x), ctx: 16 (over y, core), tensor: 8 (over z).
Axes of the slice: x: 4, y: 8, z: 8, core: 2. Of those that a mesh axis runs over, the one named last changes fastest.
Arguments:
- tokens: bfloat16 [8192, 8192], P(('dp', 'tensor'), 'ctx'), parts along dimension 0, may hold values from -6 to 6
- queries: bfloat16 [8192, 8192], P(('dp', 'ctx'), 'tensor'), parts along dimension 0, may hold values from -100 to 100
- key_value_weight: bfloat16 [8192, 2048], P('ctx', 'tensor'), may hold values from -0.0625 to 0.0625
- out_weight: bfloat16 [8192, 8192], P('tensor', 'ctx'), may hold values from -0.0625 to 0.0625
- doc_lengths: int32 [32], P('dp'), parts along dimension 0, may hold values from 1 to 1024, 2048 in all
- block_order: int32 [128], P('dp'), parts along dimension 0, may hold values from 0 to 31, each once
Outputs:
- mixed: bfloat16 [8192, 8192], P(('dp', 'tensor'), 'ctx'), parts along dimension 0
There are 4 independent parts, one for each index of `dp`. A program takes and returns all parts, laid end to end along the dimension named above; an argument that names none is the same for every part. Nothing has to cross between parts.
Inputs may be any that keep to these rules, and one draw needn't show every extreme that they name: `doc_lengths`: the lengths add up to 2048. `block_order`: each of 0 to 31 once.
All inputs are finite; a program needn't handle non-finite values.
Results may differ from a plain program's by a relative error of at most 0.014.
Values may be sent and summed in bfloat16 or wider, within the bound.
No kernel may reach another device: no remote copies, remote signals or barrier semaphores. Data moves between devices by JAX's collectives and lax.ppermute only.
A program may use at most 64 MiB of HBM per device.

v0:
```python
import math
import jax
import jax.numpy as jnp
from jax import lax
from jax.sharding import PartitionSpec as P

HEAD_WIDTH = 128


def doc_index(positions, doc_ends):
    return jnp.sum((doc_ends[None, :] <= positions[:, None]).astype(jnp.int32), axis=1)


def make_attend(query_groups, query_pos, query_doc, doc_ends):
    scale = 1.0 / jnp.sqrt(jnp.float32(HEAD_WIDTH))

    def attend(running, kv_piece, first_row):
        key_count = kv_piece.shape[0]
        key_pos = first_row + jnp.arange(key_count, dtype=jnp.int32)
        key_doc = doc_index(key_pos, doc_ends)
        allowed = (query_doc[:, None] == key_doc[None, :]) & (
            key_pos[None, :] <= query_pos[:, None]
        )

        def update(state_in):
            top_score, total, weighted = state_in
            split_kv = kv_piece.reshape(key_count, query_groups.shape[1], 2, HEAD_WIDTH)
            keys_now = split_kv[:, :, 0, :]
            values_now = split_kv[:, :, 1, :]
            scores = (
                jnp.einsum(
                    "tkgd,nkd->tkgn", query_groups, keys_now, preferred_element_type=jnp.float32
                )
                * scale
            )
            visible = allowed[:, None, None, :]
            piece_top = jnp.max(jnp.where(visible, scores, jnp.float32(-1e30)), axis=-1)
            new_top = jnp.maximum(top_score, piece_top)
            probs = jnp.where(visible, jnp.exp(scores - new_top[..., None]), jnp.float32(0.0))
            rescale = jnp.exp(top_score - new_top)
            total = total * rescale + jnp.sum(probs, axis=-1)
            weighted = weighted * rescale[..., None] + jnp.einsum(
                "tkgn,nkd->tkgd",
                probs.astype(jnp.bfloat16),
                values_now,
                preferred_element_type=jnp.float32,
            )
            return (new_top, total, weighted)

        def unchanged(state_in):
            return state_in

        return lax.cond(jnp.any(allowed), update, unchanged, running)

    return attend


def local(tokens, queries, key_value_weight, out_weight, doc_lengths, block_order):
    ctx_count = lax.axis_size("ctx")
    ctx_rank = lax.axis_index("ctx")
    local_rows = queries.shape[0]
    seq_rows = local_rows * ctx_count
    half_rows = local_rows // 2
    doc_ends = jnp.cumsum(doc_lengths)
    own_blocks = lax.dynamic_slice_in_dim(block_order, 2 * ctx_rank, 2)
    query_pos = jnp.repeat(
        own_blocks, half_rows, total_repeat_length=local_rows
    ) * half_rows + jnp.tile(jnp.arange(half_rows, dtype=jnp.int32), 2)
    query_doc = doc_index(query_pos, doc_ends)
    heads_width = queries.shape[1]
    kv_heads = key_value_weight.shape[1] // (2 * HEAD_WIDTH)
    queries_per_group = heads_width // HEAD_WIDTH // kv_heads
    query_groups = queries.reshape(local_rows, kv_heads, queries_per_group, HEAD_WIDTH)
    attend = make_attend(query_groups, query_pos, query_doc, doc_ends)
    initial = (
        jnp.full((local_rows, kv_heads, queries_per_group), -1e30, jnp.float32),
        jnp.zeros((local_rows, kv_heads, queries_per_group), jnp.float32),
        jnp.zeros((local_rows, kv_heads, queries_per_group, HEAD_WIDTH), jnp.float32),
    )
    partial_kv = jnp.dot(
        lax.all_gather(tokens, "tensor", axis=0, tiled=True),
        key_value_weight,
        preferred_element_type=jnp.float32,
    )
    whole_kv = lax.psum(partial_kv, "ctx").astype(jnp.bfloat16)
    key_step = math.gcd(seq_rows, 512)

    def visit(key_block, running):
        kv_piece = lax.dynamic_slice_in_dim(whole_kv, key_block * key_step, key_step, 0)
        return attend(running, kv_piece, key_block * key_step)

    result = lax.fori_loop(0, seq_rows // key_step, visit, initial)
    top_score, total, weighted = result
    attn = (weighted / total[..., None]).astype(jnp.bfloat16).reshape(local_rows, heads_width)
    partial_out = jnp.dot(
        lax.all_gather(attn, "ctx", axis=0, tiled=True),
        out_weight,
        preferred_element_type=jnp.float32,
    )
    mixed = lax.psum_scatter(
        partial_out.astype(jnp.bfloat16), "tensor", scatter_dimension=0, tiled=True
    )
    return mixed


def solution(mesh):
    in_specs = (
        P(("dp", "tensor"), "ctx"),
        P(("dp", "ctx"), "tensor"),
        P("ctx", "tensor"),
        P("tensor", "ctx"),
        P("dp"),
        P("dp"),
    )
    out_specs = P(("dp", "tensor"), "ctx")
    return jax.shard_map(local, mesh=mesh, in_specs=in_specs, out_specs=out_specs, check_vma=False)
```

profile of v0, /device:TPU:8, one launch (start us, length us, event | category | flops | bytes accessed | tf_op | source)
XLA Modules:
  0.0 245.9 jit_solution(3208315371400769322)
XLA Ops:
  6.5 0.0 copy-start
  6.5 0.0 all-gather.3.cloned.1.call-start
  6.5 0.7 all-gather.3.cloned.1.call-update
  7.3 0.0 all-gather.5.cloned.1.call-start
  7.3 0.8 reduce-window.10
  8.1 0.1 tile.10
  8.2 1.1 copy.16
  9.4 0.2 copy.18
  9.6 0.7 dynamic_slice.14
  10.3 0.6 fusion.21
  10.9 1.9 fusion.19
  12.8 0.1 convert_reduce_fusion.1
  12.8 45.1 %all-gather.3.cloned.1.call-done = bf16[2048,512]{1,0:T(8,128)(2,1)} async-done(((bf16[256,512]{1,0:T(8,128)(2,1)}), bf16[2048,512]{1,0:T(8,128)(2,1)}) %all-gather.3.cloned.1.call-update) | async-done | bytes 2097168 | tf_op jit(solution)/shard_map/all_gather | solution.py:81
  58.0 2.3 fusion.22
  60.3 55.5 %all-reduce.1 = bf16[2048,256]{1,0:T(8,128)(2,1)} all-reduce(f32[2048,256]{1,0:T(8,128)S(1)} %fusion.22), channel_id=1, replica_groups=mesh['dp'=4,'ctx'=16,'tensor'=8] {'ctx'}, use_global_device_ids=true, to_apply=%region_0.0 | all-reduce | flops 524288 | bytes 3145728 | tf_op jit(solution)/shard_map/psum | solution.py:85
  115.8 0.0 copy-start.1
  115.8 1.5 copy.17
  117.4 0.0 copy-done.1
  117.4 15.2 %while.19 = (s32[]{:T(128)}, f32[128,1,8]{0,2,1:T(8,128)S(1)}, f32[128,1,8]{0,2,1:T(8,128)S(1)}, f32[128,1,8,128]{0,3,2,1:T(8,128)S(1)}, s32[128]{0:T(128)S(1)},...) while((s32[]{:T(128)}, f32[128,1,8]{0,2,1:T(8,128)S(1)}, ...), condition=%wide.region_10.11_spmd.clone, body=%wide.region_3.10_spmd.clone.sunk | while | flops 274742656 | bytes 8730577 | solution.py:92
  117.4 0.1 tile.22
  117.5 1.2 multiply_add_fusion.2
  118.7 0.1 convert_reduce_fusion.3
  118.8 0.9 fusion.28
  120.3 1.7 conditional.3
  120.4 0.5 fusion.2
  120.9 0.4 fusion.6
  121.3 0.6 fusion.7
  122.0 0.1 tile.22
  122.1 1.2 multiply_add_fusion.2
  123.4 0.1 convert_reduce_fusion.3
  123.4 0.9 fusion.28
  125.0 0.1 tile.22
  125.1 1.2 multiply_add_fusion.2
  126.3 0.1 convert_reduce_fusion.3
  126.4 0.9 fusion.28
  128.0 0.1 tile.22
  128.0 1.2 multiply_add_fusion.2
  129.3 0.1 convert_reduce_fusion.3
  129.4 0.9 fusion.28
  130.9 1.7 conditional.3
  130.9 0.5 fusion.2
  131.4 0.4 fusion.6
  131.9 0.6 fusion.7
  132.6 0.8 divide_convert_fusion
  133.3 0.0 all-gather.5.cloned.1.call-update
  133.3 0.0 reduce-scatter.2.cloned.1.call-start
  133.4 54.3 %all-gather.5.cloned.1.call-done = bf16[2048,1024]{0,1:T(8,128)(2,1)} async-done(((bf16[128,1024]{0,1:T(8,128)(2,1)}), bf16[2048,1024]{0,1:T(8,128)(2,1)}) %all-gather.5.cloned.1.call-update) | async-done | bytes 4194320 | tf_op jit(solution)/shard_map/all_gather | solution.py:96
  187.6 0.0 copy-done
  187.7 5.9 %convolution_convert_fusion = bf16[2048,512]{1,0:T(8,128)(2,1)} fusion(bf16[2048,1024]{0,1:T(8,128)(2,1)} %all-gather.5.cloned.1.call-done, bf16[1024,512]{1,0:T(8,128)(2,1)S(1)} %copy-done), kind=kOutput, calls=%fused_computation.30 | convolution fusion | flops 2148532224 | bytes 7340032 | tf_op jit(solution)/shard_map/dot_general | solution.py:95
  193.5 0.0 reduce-scatter.2.cloned.1.call-update
  193.6 45.8 %reduce-scatter.2.cloned.1.call-done = bf16[256,512]{1,0:T(8,128)(2,1)} async-done(((bf16[2048,512]{1,0:T(8,128)(2,1)}), bf16[256,512]{1,0:T(8,128)(2,1)}) %reduce-scatter.2.cloned.1.call-update) | async-done | bytes 262160 | tf_op jit(solution)/shard_map/reduce_scatter | solution.py:100
  (22 shorter events, 0.2 us)
Async XLA Ops:
  6.5 181.1 %copy-start = (bf16[1024,512]{1,0:T(8,128)(2,1)S(1)}, bf16[1024,512]{1,0:T(8,128)(2,1)}, u32[]{:S(2)}) copy-start(bf16[1024,512]{1,0:T(8,128)(2,1)} %param.15) | copy-start | bytes 3145732
  6.5 51.5 %all-gather.3.cloned.1.call-start = ((), (), s32[]{:S(2)}) async-start(), calls=%async_computation.1 | async-start | bytes 2359296 | tf_op jit(solution)/shard_map/all_gather | solution.py:81
  7.3 180.4 %all-gather.5.cloned.1.call-start = ((), (), s32[]{:S(2)}) async-start(), calls=%async_computation.2 | async-start | bytes 4456448 | tf_op jit(solution)/shard_map/all_gather | solution.py:96
  115.8 1.6 copy-start.1
  133.3 106.0 %reduce-scatter.2.cloned.1.call-start = ((), (), s32[]{:S(2)}) async-start(), calls=%async_computation.3 | async-start | bytes 2359296 | tf_op jit(solution)/shard_map/reduce_scatter | solution.py:100
Sparse Core Ops, SparseCore 0:
  9.4 48.5 all-gather.2
  133.5 54.1 all-gather.4
  193.7 45.6 reduce-scatter.1
where the time goes:
time: 246 us
  waiting for transfers between devices  146 us (59%)
  blocking collectives  55.5 us (23%)
  other arithmetic  13.2 us (5%)
  between operations  13.2 us (5%)
  matrix products  10.4 us (4%)
  local copies, waits for them, and re-layouts  4.66 us (2%)
  loops' own time  2.91 us (1%)
    psum x1, blocking collectives, local(): whole_kv = lax.psum(partial_kv, 'ctx').astype(jnp.bfloat16)  55.5 us
    all_gather x1, waiting for transfers between devices, local(): lax.all_gather(attn, 'ctx', axis=0, tiled=True)  54.3 us
    reduce_scatter x1, waiting for transfers between devices, local(): lax.psum_scatter(partial_out.astype(jnp.bfloat16), 'tensor', scatter_dime...  45.8 us
    all_gather x1, waiting for transfers between devices, local(): lax.all_gather(tokens, 'tensor', axis=0, tiled=True)  45.1 us
    add x5, other arithmetic, local(): jnp.repeat(own_blocks, half_rows, total_repeat_length=local_rows)  6.79 us
    dot_general x1, matrix products, local(): jnp.dot(lax.all_gather(attn, 'ctx', axis=0, tiled=True), out_weight, pref...  5.9 us
  transfers between devices with their start and end apart: 3, of which 3 were waited for; matrix products, arithmetic and copies ran while one was open for 2% of the time, Pallas kernels for 0%

commit v1 on v0

--- a/solution.py
+++ b/solution.py
@@ -5,6 +5,28 @@
 from jax.sharding import PartitionSpec as P
 
 HEAD_WIDTH = 128
+
+
+def in_order(parts, dim):
+    parts = jnp.moveaxis(parts, 0, dim)
+    lengths = parts.shape
+    return parts.reshape(*lengths[:dim], lengths[dim] * lengths[dim + 1], *lengths[dim + 2 :])
+
+
+def ring_gather(x, axis, dim):
+    size = lax.axis_size(axis)
+    pairs = [(i, (i + 1) % size) for i in range(size)]
+    back = [(b, a) for a, b in pairs]
+    lower, upper = ([], [])
+    for step in range(size - 1):
+        if step % 2 == 0:
+            lower.append(lax.ppermute(lower[-1] if lower else x, axis, pairs))
+        else:
+            upper.append(lax.ppermute(upper[-1] if upper else x, axis, back))
+    parts = jnp.stack([*lower[::-1], x, *upper])
+    shift = lax.axis_index(axis) - len(lower)
+    parts = parts[(jnp.arange(size) - shift) % size]
+    return in_order(parts, dim)
 
 
 def doc_index(positions, doc_ends):
@@ -93,9 +115,7 @@
     top_score, total, weighted = result
     attn = (weighted / total[..., None]).astype(jnp.bfloat16).reshape(local_rows, heads_width)
     partial_out = jnp.dot(
-        lax.all_gather(attn, "ctx", axis=0, tiled=True),
-        out_weight,
-        preferred_element_type=jnp.float32,
+        ring_gather(attn, "ctx", 0), out_weight, preferred_element_type=jnp.float32
     )
     mixed = lax.psum_scatter(
         partial_out.astype(jnp.bfloat16), "tensor", scatter_dimension=0, tiled=True

time: 246 us -> 276 us (1.12)
  the two profiles are of different devices: /device:TPU:8 before, /device:TPU:10 now
where the time goes in v1:
time: 276 us; the launch traced here: 275 us
  waiting for transfers between devices  134 us (49%)
  blocking collectives  55.5 us (20%)
  local copies, waits for them, and re-layouts  28.2 us (10%)
  starting transfers between devices  17.9 us (6%)
  between operations  13.6 us (5%)
  other arithmetic  13.1 us (5%)
  matrix products  10.4 us (4%)
  loops' own time  2.89 us (1%)
    psum x1, blocking collectives, local(): whole_kv = lax.psum(partial_kv, 'ctx').astype(jnp.bfloat16)  55.5 us
    reduce_scatter x1, waiting for transfers between devices, local(): lax.psum_scatter(partial_out.astype(jnp.bfloat16), 'tensor', scatter_dime...  54.3 us
    all_gather x1, waiting for transfers between devices, local(): lax.all_gather(tokens, 'tensor', axis=0, tiled=True)  44.9 us
    ppermute x8, waiting for transfers between devices, ring_gather(): lower.append(lax.ppermute(lower[-1] if lower else x, axis, pairs))  33.5 us
    unnamed x28, local copies, waits for them, and re-layouts  20.3 us
    ppermute x7, starting transfers between devices, ring_gather(): upper.append(lax.ppermute(upper[-1] if upper else x, axis, back))  17.8 us
    add x5, other arithmetic, local(): jnp.repeat(own_blocks, half_rows, total_repeat_length=local_rows)  7.41 us
    dot_general x1, matrix products, local(): jnp.dot(ring_gather(attn, 'ctx', 0), out_weight, preferred_element_type=j...  5.87 us
  transfers between devices with their start and end apart: 17, of which 11 were waited for; matrix products, arithmetic and copies ran while one was open for 8% of the time, Pallas kernels for 0%

profile of v1, /device:TPU:10, one launch (start us, length us, event | category | flops | bytes accessed | tf_op | source)
XLA Modules:
  0.0 275.2 jit_solution(11481335622086058192)
XLA Ops:
  6.5 0.7 all-gather.2.cloned.1.call-update
  7.4 0.8 reduce-window.10
  8.2 1.1 copy.23
  9.4 0.2 copy.25
  9.5 0.7 dynamic_slice.14
  10.3 0.6 fusion.23
  10.9 2.0 fusion.21
  13.0 44.9 %all-gather.2.cloned.1.call-done = bf16[2048,512]{1,0:T(8,128)(2,1)} async-done(((bf16[256,512]{1,0:T(8,128)(2,1)}), bf16[2048,512]{1,0:T(8,128)(2,1)}) %all-gather.2.cloned.1.call-update) | async-done | bytes 2097168 | tf_op jit(solution)/shard_map/all_gather | solution.py:103
  58.0 2.3 fusion.24
  60.3 55.5 %all-reduce.1 = bf16[2048,256]{1,0:T(8,128)(2,1)} all-reduce(f32[2048,256]{1,0:T(8,128)S(1)} %fusion.24), channel_id=1, replica_groups=mesh['dp'=4,'ctx'=16,'tensor'=8] {'ctx'}, use_global_device_ids=true, to_apply=%region_0.0 | all-reduce | flops 524288 | bytes 3145728 | tf_op jit(solution)/shard_map/psum | solution.py:107
  115.8 1.5 copy.24
  117.4 15.7 %while.19 = (s32[]{:T(128)}, f32[128,1,8]{0,2,1:T(8,128)S(1)}, f32[128,1,8]{0,2,1:T(8,128)S(1)}, f32[128,1,8,128]{0,3,2,1:T(8,128)S(1)}, s32[128]{0:T(128)S(1)},...) while((s32[]{:T(128)}, f32[128,1,8]{0,2,1:T(8,128)S(1)}, ...), condition=%wide.region_10.11_spmd.clone, body=%wide.region_3.10_spmd.clone.sunk | while | flops 274742656 | bytes 8730577 | solution.py:114
  117.6 1.4 multiply_add_fusion.2
  118.9 0.9 fusion.30
  120.6 1.4 multiply_add_fusion.2
  122.0 0.9 fusion.30
  123.5 1.7 conditional.3
  123.6 0.5 fusion.2
  124.1 0.6 fusion.7
  124.7 0.4 fusion.6
  125.4 1.4 multiply_add_fusion.2
  126.7 0.9 fusion.30
  128.2 1.7 conditional.3
  128.3 0.5 fusion.2
  128.8 0.6 fusion.7
  129.5 0.4 fusion.6
  130.1 1.4 multiply_add_fusion.2
  131.5 0.9 fusion.30
  133.1 0.1 copy.29
  133.3 5.8 %collective-permute-done = bf16[128,1024]{1,0:T(8,128)(2,1)S(1)} collective-permute-done((bf16[128,1024]{1,0:T(8,128)(2,1)S(1)}, bf16[128,1024]{1,0:T(8,128)(2,1)S(1)}, u32[]{:S(2)}, u32[]{:S(2)}) %collective-permute-start) | collective-permute-done | bytes 262176 | tf_op jit(solution)/shard_map/ppermute | solution.py:23
  139.0 1.7 collective-permute-start.8
  140.8 4.1 %collective-permute-done.1 = bf16[128,1024]{1,0:T(8,128)(2,1)S(1)} collective-permute-done((bf16[128,1024]{1,0:T(8,128)(2,1)S(1)}, bf16[128,1024]{1,0:T(8,128)(2,1)S(1)}, u32[]{:S(2)}, u32[]{:S(2)}) %collective-permute-start.1) | collective-permute-done | bytes 262176 | tf_op jit(solution)/shard_map/ppermute | solution.py:23
  144.8 1.7 collective-permute-start.9
  146.6 4.0 %collective-permute-done.2 = bf16[128,1024]{1,0:T(8,128)(2,1)S(1)} collective-permute-done((bf16[128,1024]{1,0:T(8,128)(2,1)S(1)}, bf16[128,1024]{1,0:T(8,128)(2,1)S(1)}, u32[]{:S(2)}, u32[]{:S(2)}) %collective-permute-start.2) | collective-permute-done | bytes 262176 | tf_op jit(solution)/shard_map/ppermute | solution.py:23
  150.6 1.9 collective-permute-start.10
  152.6 3.9 %collective-permute-done.3 = bf16[128,1024]{1,0:T(8,128)(2,1)S(1)} collective-permute-done((bf16[128,1024]{1,0:T(8,128)(2,1)S(1)}, bf16[128,1024]{1,0:T(8,128)(2,1)S(1)}, u32[]{:S(2)}, u32[]{:S(2)}) %collective-permute-start.3) | collective-permute-done | bytes 262176 | tf_op jit(solution)/shard_map/ppermute | solution.py:23
  156.5 3.1 %collective-permute-start.11 = (bf16[128,1024]{1,0:T(8,128)(2,1)S(1)}, bf16[128,1024]{1,0:T(8,128)(2,1)S(1)}, u32[]{:S(2)}, u32[]{:S(2)}) collective-permute-start(bf16[128,1024]{1,0:T(8,128)(2,1)S(1)} %collective-permute-done.10), channel_id=1, source_target_pairs={{8,0},{16,8},{24,16},{32,24},{40,32},{48,40},{56,48},{64,56},{72,6... | collective-permute-start | bytes 786440 | tf_op jit(solution)/shard_map/ppermute | solution.py:25
  159.6 3.9 %collective-permute-done.4 = bf16[128,1024]{1,0:T(8,128)(2,1)S(1)} collective-permute-done((bf16[128,1024]{1,0:T(8,128)(2,1)S(1)}, bf16[128,1024]{1,0:T(8,128)(2,1)S(1)}, u32[]{:S(2)}, u32[]{:S(2)}) %collective-permute-start.4) | collective-permute-done | bytes 262176 | tf_op jit(solution)/shard_map/ppermute | solution.py:23
  163.5 3.1 %collective-permute-start.12 = (bf16[128,1024]{1,0:T(8,128)(2,1)S(1)}, bf16[128,1024]{1,0:T(8,128)(2,1)}, u32[]{:S(2)}, u32[]{:S(2)}) collective-permute-start(bf16[128,1024]{1,0:T(8,128)(2,1)S(1)} %collective-permute-done.11), channel_id=1, source_target_pairs={{8,0},{16,8},{24,16},{32,24},{40,32},{48,40},{56,48},{64,56},{72,6... | collective-permute-start | bytes 786440 | tf_op jit(solution)/shard_map/ppermute | solution.py:25
  166.6 3.9 %collective-permute-done.5 = bf16[128,1024]{1,0:T(8,128)(2,1)S(1)} collective-permute-done((bf16[128,1024]{1,0:T(8,128)(2,1)S(1)}, bf16[128,1024]{1,0:T(8,128)(2,1)S(1)}, u32[]{:S(2)}, u32[]{:S(2)}) %collective-permute-start.5) | collective-permute-done | bytes 262176 | tf_op jit(solution)/shard_map/ppermute | solution.py:23
  170.5 3.2 %collective-permute-start.13 = (bf16[128,1024]{1,0:T(8,128)(2,1)}, bf16[128,1024]{1,0:T(8,128)(2,1)}, u32[]{:S(2)}, u32[]{:S(2)}) collective-permute-start(bf16[128,1024]{1,0:T(8,128)(2,1)} %collective-permute-done.12), channel_id=1, source_target_pairs={{8,0},{16,8},{24,16},{32,24},{40,32},{48,40},{56,48},{64,56},{72,6... | collective-permute-start | bytes 786440 | tf_op jit(solution)/shard_map/ppermute | solution.py:25
  173.8 3.9 %collective-permute-done.6 = bf16[128,1024]{1,0:T(8,128)(2,1)} collective-permute-done((bf16[128,1024]{1,0:T(8,128)(2,1)S(1)}, bf16[128,1024]{1,0:T(8,128)(2,1)}, u32[]{:S(2)}, u32[]{:S(2)}) %collective-permute-start.6) | collective-permute-done | bytes 262176 | tf_op jit(solution)/shard_map/ppermute | solution.py:23
  177.8 0.1 collective-permute-done.13
  178.0 3.0 %collective-permute-start.14 = (bf16[128,1024]{1,0:T(8,128)(2,1)}, bf16[128,1024]{1,0:T(8,128)(2,1)S(1)}, u32[]{:S(2)}, u32[]{:S(2)}) collective-permute-start(bf16[128,1024]{1,0:T(8,128)(2,1)} %collective-permute-done.13), channel_id=1, source_target_pairs={{8,0},{16,8},{24,16},{32,24},{40,32},{48,40},{56,48},{64,56},{72,6... | collective-permute-start | bytes 786440 | tf_op jit(solution)/shard_map/ppermute | solution.py:25
  181.0 4.0 %collective-permute-done.7 = bf16[128,1024]{1,0:T(8,128)(2,1)} collective-permute-done((bf16[128,1024]{1,0:T(8,128)(2,1)}, bf16[128,1024]{1,0:T(8,128)(2,1)}, u32[]{:S(2)}, u32[]{:S(2)}) %collective-permute-start.7) | collective-permute-done | bytes 262176 | tf_op jit(solution)/shard_map/ppermute | solution.py:23
  185.0 1.7 bitcast_dynamic-update-slice_fusion.14
  186.7 1.7 bitcast_dynamic-update-slice_fusion.13
  188.3 1.7 bitcast_dynamic-update-slice_fusion.12
  190.0 1.7 bitcast_dynamic-update-slice_fusion.11
  191.7 1.7 bitcast_dynamic-update-slice_fusion.10
  193.3 0.7 bitcast_dynamic-update-slice_fusion.9
  194.1 0.7 bitcast_dynamic-update-slice_fusion.8
  194.8 0.7 bitcast_dynamic-update-slice_fusion.7
  195.5 0.7 constant_dynamic-update-slice_fusion
  196.2 0.7 bitcast_dynamic-update-slice_fusion.6
  197.0 0.7 bitcast_dynamic-update-slice_fusion.5
  197.7 0.7 bitcast_dynamic-update-slice_fusion.4
  198.4 0.7 bitcast_dynamic-update-slice_fusion.3
  199.1 1.7 bitcast_dynamic-update-slice_fusion.2
  200.8 1.7 bitcast_dynamic-update-slice_fusion.1
  202.5 0.7 bitcast_dynamic-update-slice_fusion
  203.2 5.0 %gather_fusion = bf16[16,128,1024]{2,1,0:T(8,128)(2,1)} fusion(bf16[16,128,1024]{2,1,0:T(8,128)(2,1)} %bitcast_dynamic-update-slice_fusion, s32[1024]{0:T(1024)S(1)} %pad_clamp_fusion), kind=kCustom, calls=%fused_computation | custom fusion | bytes 8388672 | tf_op jit(solution)/shard_map/gather | solution.py:28
  208.2 5.9 %convolution_convert_fusion = bf16[2048,512]{1,0:T(8,128)(2,1)} fusion(bf16[2048,1024]{1,0:T(8,128)(2,1)} %bitcast.101, bf16[1024,512]{1,0:T(8,128)(2,1)S(1)} %copy-done), kind=kOutput, calls=%fused_computation.31 | convolution fusion | flops 2148532224 | bytes 7340032 | tf_op jit(solution)/shard_map/dot_general | solution.py:117
  214.0 54.3 %reduce-scatter.2.cloned.1.call-done = bf16[256,512]{1,0:T(8,128)(2,1)} async-done(((bf16[2048,512]{1,0:T(8,128)(2,1)}), bf16[256,512]{1,0:T(8,128)(2,1)}) %reduce-scatter.2.cloned.1.call-update) | async-done | bytes 262160 | tf_op jit(solution)/shard_map/reduce_scatter | solution.py:120
  (63 shorter events, 1.4 us)
Async XLA Ops:
  6.5 201.6 %copy-start = (bf16[1024,512]{1,0:T(8,128)(2,1)S(1)}, bf16[1024,512]{1,0:T(8,128)(2,1)}, u32[]{:S(2)}) copy-start(bf16[1024,512]{1,0:T(8,128)(2,1)} %param.15) | copy-start | bytes 3145732
  6.5 51.4 %all-gather.2.cloned.1.call-start = ((), (), s32[]{:S(2)}) async-start(), calls=%async_computation.1 | async-start | bytes 2359296 | tf_op jit(solution)/shard_map/all_gather | solution.py:103
  7.3 261.1 %reduce-scatter.2.cloned.1.call-start = ((), (), s32[]{:S(2)}) async-start(), calls=%async_computation.2 | async-start | bytes 2359296 | tf_op jit(solution)/shard_map/reduce_scatter | solution.py:120
  60.3 57.1 %copy-start.4 = (pred[128]{0:T(512)(128)(4,1)S(1)}, pred[128]{0:T(512)(128)(4,1)}, u32[]{:S(2)}) copy-start(pred[128]{0:T(512)(128)(4,1)} %constant.181) | copy-start | bytes 388
  133.2 5.8 %collective-permute-start = (bf16[128,1024]{1,0:T(8,128)(2,1)S(1)}, bf16[128,1024]{1,0:T(8,128)(2,1)S(1)}, u32[]{:S(2)}, u32[]{:S(2)}) collective-permute-start(bf16[128,1024]{1,0:T(8,128)(2,1)S(1)} %copy.29), channel_id=1, source_target_pairs={{0,8},{8,16},{16,24},{24,32},{32,40},{40,48},{48,56},{56,64},{64,7... | collective-permute-start | bytes 786440 | tf_op jit(solution)/shard_map/ppermute | solution.py:23
  139.0 5.8 %collective-permute-start.1 = (bf16[128,1024]{1,0:T(8,128)(2,1)S(1)}, bf16[128,1024]{1,0:T(8,128)(2,1)S(1)}, u32[]{:S(2)}, u32[]{:S(2)}) collective-permute-start(bf16[128,1024]{1,0:T(8,128)(2,1)S(1)} %collective-permute-done), channel_id=1, source_target_pairs={{0,8},{8,16},{16,24},{24,32},{32,40},{40,48},{48,56},{56,64},{64,7... | collective-permute-start | bytes 786440 | tf_op jit(solution)/shard_map/ppermute | solution.py:23
  139.0 5.8 %collective-permute-start.8 = (bf16[128,1024]{1,0:T(8,128)(2,1)S(1)}, bf16[128,1024]{1,0:T(8,128)(2,1)S(1)}, u32[]{:S(2)}, u32[]{:S(2)}) collective-permute-start(bf16[128,1024]{1,0:T(8,128)(2,1)S(1)} %copy.29), channel_id=1, source_target_pairs={{8,0},{16,8},{24,16},{32,24},{40,32},{48,40},{56,48},{64,56},{72,6... | collective-permute-start | bytes 786440 | tf_op jit(solution)/shard_map/ppermute | solution.py:25
  144.8 5.8 %collective-permute-start.2 = (bf16[128,1024]{1,0:T(8,128)(2,1)S(1)}, bf16[128,1024]{1,0:T(8,128)(2,1)S(1)}, u32[]{:S(2)}, u32[]{:S(2)}) collective-permute-start(bf16[128,1024]{1,0:T(8,128)(2,1)S(1)} %collective-permute-done.1), channel_id=1, source_target_pairs={{0,8},{8,16},{16,24},{24,32},{32,40},{40,48},{48,56},{56,64},{64,7... | collective-permute-start | bytes 786440 | tf_op jit(solution)/shard_map/ppermute | solution.py:23
  144.8 5.8 %collective-permute-start.9 = (bf16[128,1024]{1,0:T(8,128)(2,1)S(1)}, bf16[128,1024]{1,0:T(8,128)(2,1)S(1)}, u32[]{:S(2)}, u32[]{:S(2)}) collective-permute-start(bf16[128,1024]{1,0:T(8,128)(2,1)S(1)} %collective-permute-done.8), channel_id=1, source_target_pairs={{8,0},{16,8},{24,16},{32,24},{40,32},{48,40},{56,48},{64,56},{72,6... | collective-permute-start | bytes 786440 | tf_op jit(solution)/shard_map/ppermute | solution.py:25
  150.6 5.9 %collective-permute-start.3 = (bf16[128,1024]{1,0:T(8,128)(2,1)S(1)}, bf16[128,1024]{1,0:T(8,128)(2,1)S(1)}, u32[]{:S(2)}, u32[]{:S(2)}) collective-permute-start(bf16[128,1024]{1,0:T(8,128)(2,1)S(1)} %collective-permute-done.2), channel_id=1, source_target_pairs={{0,8},{8,16},{16,24},{24,32},{32,40},{40,48},{48,56},{56,64},{64,7... | collective-permute-start | bytes 786440 | tf_op jit(solution)/shard_map/ppermute | solution.py:23
  150.6 5.9 %collective-permute-start.10 = (bf16[128,1024]{1,0:T(8,128)(2,1)S(1)}, bf16[128,1024]{1,0:T(8,128)(2,1)S(1)}, u32[]{:S(2)}, u32[]{:S(2)}) collective-permute-start(bf16[128,1024]{1,0:T(8,128)(2,1)S(1)} %collective-permute-done.9), channel_id=1, source_target_pairs={{8,0},{16,8},{24,16},{32,24},{40,32},{48,40},{56,48},{64,56},{72,6... | collective-permute-start | bytes 786440 | tf_op jit(solution)/shard_map/ppermute | solution.py:25
  156.5 14.0 %copy-start.1 = (bf16[128,1024]{1,0:T(8,128)(2,1)}, bf16[128,1024]{1,0:T(8,128)(2,1)S(1)}, u32[]{:S(2)}) copy-start(bf16[128,1024]{1,0:T(8,128)(2,1)S(1)} %collective-permute-done.3) | copy-start | bytes 786436
  156.5 7.0 %collective-permute-start.4 = (bf16[128,1024]{1,0:T(8,128)(2,1)S(1)}, bf16[128,1024]{1,0:T(8,128)(2,1)S(1)}, u32[]{:S(2)}, u32[]{:S(2)}) collective-permute-start(bf16[128,1024]{1,0:T(8,128)(2,1)S(1)} %collective-permute-done.3), channel_id=1, source_target_pairs={{0,8},{8,16},{16,24},{24,32},{32,40},{40,48},{48,56},{56,64},{64,7... | collective-permute-start | bytes 786440 | tf_op jit(solution)/shard_map/ppermute | solution.py:23
  156.5 7.0 %collective-permute-start.11 = (bf16[128,1024]{1,0:T(8,128)(2,1)S(1)}, bf16[128,1024]{1,0:T(8,128)(2,1)S(1)}, u32[]{:S(2)}, u32[]{:S(2)}) collective-permute-start(bf16[128,1024]{1,0:T(8,128)(2,1)S(1)} %collective-permute-done.10), channel_id=1, source_target_pairs={{8,0},{16,8},{24,16},{32,24},{40,32},{48,40},{56,48},{64,56},{72,6... | collective-permute-start | bytes 786440 | tf_op jit(solution)/shard_map/ppermute | solution.py:25
  163.5 10.3 %copy-start.2 = (bf16[128,1024]{1,0:T(8,128)(2,1)}, bf16[128,1024]{1,0:T(8,128)(2,1)S(1)}, u32[]{:S(2)}) copy-start(bf16[128,1024]{1,0:T(8,128)(2,1)S(1)} %collective-permute-done.4) | copy-start | bytes 786436
  163.5 7.0 %collective-permute-start.5 = (bf16[128,1024]{1,0:T(8,128)(2,1)S(1)}, bf16[128,1024]{1,0:T(8,128)(2,1)S(1)}, u32[]{:S(2)}, u32[]{:S(2)}) collective-permute-start(bf16[128,1024]{1,0:T(8,128)(2,1)S(1)} %collective-permute-done.4), channel_id=1, source_target_pairs={{0,8},{8,16},{16,24},{24,32},{32,40},{40,48},{48,56},{56,64},{64,7... | collective-permute-start | bytes 786440 | tf_op jit(solution)/shard_map/ppermute | solution.py:23
  163.5 7.0 %collective-permute-start.12 = (bf16[128,1024]{1,0:T(8,128)(2,1)S(1)}, bf16[128,1024]{1,0:T(8,128)(2,1)}, u32[]{:S(2)}, u32[]{:S(2)}) collective-permute-start(bf16[128,1024]{1,0:T(8,128)(2,1)S(1)} %collective-permute-done.11), channel_id=1, source_target_pairs={{8,0},{16,8},{24,16},{32,24},{40,32},{48,40},{56,48},{64,56},{72,6... | collective-permute-start | bytes 786440 | tf_op jit(solution)/shard_map/ppermute | solution.py:25
  170.5 7.1 %copy-start.3 = (bf16[128,1024]{1,0:T(8,128)(2,1)}, bf16[128,1024]{1,0:T(8,128)(2,1)S(1)}, u32[]{:S(2)}) copy-start(bf16[128,1024]{1,0:T(8,128)(2,1)S(1)} %collective-permute-done.5) | copy-start | bytes 786436
  170.5 7.1 %collective-permute-start.6 = (bf16[128,1024]{1,0:T(8,128)(2,1)S(1)}, bf16[128,1024]{1,0:T(8,128)(2,1)}, u32[]{:S(2)}, u32[]{:S(2)}) collective-permute-start(bf16[128,1024]{1,0:T(8,128)(2,1)S(1)} %collective-permute-done.5), channel_id=1, source_target_pairs={{0,8},{8,16},{16,24},{24,32},{32,40},{40,48},{48,56},{56,64},{64,7... | collective-permute-start | bytes 786440 | tf_op jit(solution)/shard_map/ppermute | solution.py:23
  170.5 7.4 %collective-permute-start.13 = (bf16[128,1024]{1,0:T(8,128)(2,1)}, bf16[128,1024]{1,0:T(8,128)(2,1)}, u32[]{:S(2)}, u32[]{:S(2)}) collective-permute-start(bf16[128,1024]{1,0:T(8,128)(2,1)} %collective-permute-done.12), channel_id=1, source_target_pairs={{8,0},{16,8},{24,16},{32,24},{40,32},{48,40},{56,48},{64,56},{72,6... | collective-permute-start | bytes 786440 | tf_op jit(solution)/shard_map/ppermute | solution.py:25
  177.6 7.4 %collective-permute-start.7 = (bf16[128,1024]{1,0:T(8,128)(2,1)}, bf16[128,1024]{1,0:T(8,128)(2,1)}, u32[]{:S(2)}, u32[]{:S(2)}) collective-permute-start(bf16[128,1024]{1,0:T(8,128)(2,1)} %collective-permute-done.6), channel_id=1, source_target_pairs={{0,8},{8,16},{16,24},{24,32},{32,40},{40,48},{48,56},{56,64},{64,7... | collective-permute-start | bytes 786440 | tf_op jit(solution)/shard_map/ppermute | solution.py:23
  178.0 24.5 %collective-permute-start.14 = (bf16[128,1024]{1,0:T(8,128)(2,1)}, bf16[128,1024]{1,0:T(8,128)(2,1)S(1)}, u32[]{:S(2)}, u32[]{:S(2)}) collective-permute-start(bf16[128,1024]{1,0:T(8,128)(2,1)} %collective-permute-done.13), channel_id=1, source_target_pairs={{8,0},{16,8},{24,16},{32,24},{40,32},{48,40},{56,48},{64,56},{72,6... | collective-permute-start | bytes 786440 | tf_op jit(solution)/shard_map/ppermute | solution.py:25
Sparse Core Ops, SparseCore 0:
  9.4 48.5 all-gather.1
  214.2 54.1 reduce-scatter.1
